TPU v7x, 256 devices: a whole 4x4x8 slice. The times are simulated.
256 devices in a mesh: plane: 8 (over x, core), row: 32 (over z, y).
Axes of the slice: x: 4, y: 4, z: 8, core: 2. Of those that a mesh axis runs over, the one named last changes fastest.
Arguments:
- image: float32 [2, 2048, 2048], P(None, 'row'), may hold values from -6 to 6
- w_planes: float32 [8], P('plane'), may hold values from -200 to 200
- owner: int32 [8, 1024, 1], P('plane'), may hold values from 0 to 31; in each aligned block of 32 rows (0 to 31, 32 to 63, ..., all dimensions but the last counted through in order) at most 2 rows name the same one
- positions: int32 [8, 2, 2048, 256], P('plane', None, 'row'), may hold values from 0 to 7295
- weights: float32 [8, 2048, 256], P('plane', 'row'), may hold values from 0.2 to 2
- counts: int32 [8, 2048], P('plane', 'row'), may hold values from 64 to 256, as said below
Outputs:
- normal_image: float32 [2, 2048, 2048], P(None, 'row', 'plane')
Inputs may be any that keep to these rules, and one draw needn't show every extreme that they name: In every plane the 32 tiles of one source index give no owner more than 2 of them; every owner is used somewhere. `counts`: slots that no tile fills are ignored; in every plane some slots have exactly 256.
All inputs are finite; a program needn't handle non-finite values.
Results may differ from a plain program's by a relative error of at most 0.0075.
Values may be sent and summed in bfloat16 or wider, within the bound.
A program may use at most 64 MiB of HBM per device.

v0:
```python
import functools

import jax
import jax.numpy as jnp
import ml_dtypes
import numpy as np
from jax import lax
from jax.experimental import pallas as pl
from jax.experimental.pallas import tpu as pltpu
from jax.sharding import PartitionSpec as P

TILE = 64
S = 8
OVER = 128
V = 256
FIELD_SPAN = 0.7
EXTENT = 2048
ROWS = 32
PLANES = 8
SCALE = 1.0 / 2048.0
TAP_RATE = -4.0 * 1.4426950408889634
MESH = pl.DeviceIdType.MESH
F32 = jnp.float32
BF16 = jnp.bfloat16
ROOT = 0.7071067811865476
SIN_POLY = (6.283184916495429, -41.34158923268831, 81.59994332977428, -76.61447253115396, 41.342882354135696, -12.471243534350362)
COS_POLY = (0.9999999890590228, -19.739204499453827, 64.9391174598908, -85.45013953079768, 60.16763095026347, -25.967599245923736, 6.52865815775625)


def host_tables():
    index = np.arange(256)
    angle = 2.0 * np.pi / 256.0 * (index[:, None] * index[None, :] % 256)
    cosine, sine = np.cos(angle), np.sin(angle)
    table = np.block([[cosine, sine], [-sine, cosine]]).astype(ml_dtypes.bfloat16)
    turn = 2.0 * np.pi / 2048.0 * (np.arange(8)[:, None] * index[None, :])
    return table, np.stack([np.cos(turn), np.sin(turn)]).astype(np.float32)


def dft4(re, im):
    ar, ai, br, bi = re[0] + re[2], im[0] + im[2], re[0] - re[2], im[0] - im[2]
    cr, ci, dr, di = re[1] + re[3], im[1] + im[3], re[1] - re[3], im[1] - im[3]
    return [ar + cr, br - di, ar - cr, br + di], [ai + ci, bi + dr, ai - ci, bi - dr]


def dft8(re, im):
    er, ei = dft4(re[0::2], im[0::2])
    od, oi = dft4(re[1::2], im[1::2])
    tr = [od[0], (od[1] - oi[1]) * ROOT, -oi[2], (od[3] + oi[3]) * -ROOT]
    ti = [oi[0], (od[1] + oi[1]) * ROOT, od[2], (od[3] - oi[3]) * ROOT]
    return [er[k] + tr[k] for k in range(4)] + [er[k] - tr[k] for k in range(4)], [
        ei[k] + ti[k] for k in range(4)
    ] + [ei[k] - ti[k] for k in range(4)]


def swap_halves(value):
    return pltpu.roll(value, 64, 1)


def screen_of(turns):
    part = turns - jnp.round(turns)
    square = part * part
    sine = jnp.full_like(part, SIN_POLY[-1])
    for term in SIN_POLY[-2::-1]:
        sine = sine * square + term
    cosine = jnp.full_like(part, COS_POLY[-1])
    for term in COS_POLY[-2::-1]:
        cosine = cosine * square + term
    return cosine * SCALE, sine * part * SCALE


def chunk_screen(w, row_start, col_start):
    spacing = FIELD_SPAN / EXTENT
    rows = lax.broadcasted_iota(jnp.int32, (16, 128), 0) + (row_start - EXTENT // 2)
    cols = lax.broadcasted_iota(jnp.int32, (16, 128), 1) + (col_start - EXTENT // 2)
    rows = rows.astype(F32) * spacing
    cols = cols.astype(F32) * spacing
    elevation = jnp.sqrt(1.0 - rows * rows - cols * cols) - 1.0
    return screen_of(w * elevation)


def spread_out(load, twiddle, stacked):
    def step(block, carry):
        rows = pl.ds(pl.multiple_of(block * 16, 16), 16)
        for half in range(2):
            pairs = load(block, rows, half)
            re, im = dft8([pair[0] for pair in pairs], [pair[1] for pair in pairs])
            lanes = slice(128 * half, 128 * half + 128)
            other = slice(256 + 128 * half, 384 + 128 * half)
            for q in range(8):
                if q == 0:
                    real, imag = re[0], im[0]
                else:
                    cosine, sine = twiddle[0, q : q + 1, lanes], twiddle[1, q : q + 1, lanes]
                    real, imag = re[q] * cosine - im[q] * sine, re[q] * sine + im[q] * cosine
                stacked[q, rows, lanes] = real.astype(BF16)
                stacked[q, rows, other] = imag.astype(BF16)
        return carry

    lax.fori_loop(0, 4, step, 0)


def turn_blocks(stacked, table, blocks):
    matrix = table[...]
    for pair in range(4):
        left = stacked[2 * pair : 2 * pair + 2].reshape(128, 512)
        out = jnp.dot(left, matrix, preferred_element_type=F32)
        for half in range(2):
            real, imag = slice(128 * half, 128 * half + 128), slice(256 + 128 * half, 384 + 128 * half)
            turned = []
            for item in range(2):
                rows = slice(64 * item, 64 * item + 64)
                square = jnp.concatenate([out[rows, real], out[rows, imag]], axis=0)
                turned.append(jnp.transpose(square).reshape(16, 8, 128))
            both = jnp.concatenate(turned, axis=1).astype(BF16)
            blocks[16 * half : 16 * half + 16, 16 * pair : 16 * pair + 16, :] = both


def gather_blocks(blocks, table, twiddle, middle):
    matrix = table[...]
    for pair in range(4):
        rows = blocks[:, 16 * pair : 16 * pair + 16, :].astype(F32)
        for item in range(2):
            q = 2 * pair + item
            flat = rows[:, 8 * item : 8 * item + 8, :].reshape(256, 128)
            low = jnp.transpose(flat[0:128]).astype(BF16)
            high = jnp.transpose(flat[128:256]).astype(BF16)
            left = jnp.concatenate([low[0:64], high[0:64], low[64:128], high[64:128]], axis=1)
            out = jnp.dot(left, matrix, preferred_element_type=F32)
            real, imag = out[:, 0:256], out[:, 256:512]
            if q:
                cosine, sine = twiddle[0, q : q + 1, :], twiddle[1, q : q + 1, :]
                real, imag = real * cosine - imag * sine, real * sine + imag * cosine
            middle[q, :, 0:256] = real
            middle[q, :, 256:512] = imag


def gather_last(middle, emit):
    def step(block, carry):
        rows = pl.ds(pl.multiple_of(block * 16, 16), 16)
        for half in range(2):
            lanes = slice(128 * half, 128 * half + 128)
            other = slice(256 + 128 * half, 384 + 128 * half)
            re, im = dft8([middle[q, rows, lanes] for q in range(8)], [middle[q, rows, other] for q in range(8)])
            emit(block, rows, half, re, im)
        return carry

    lax.fori_loop(0, 4, step, 0)


def low_lanes():
    return lax.broadcasted_iota(jnp.int32, (16, 128), 1) < 64


def load_received(blocks):
    def load(block, rows, half):
        low = low_lanes()
        pairs = []
        for a in range(8):
            first = blocks[4 * a + 2 * half, rows, :].astype(F32)
            second = blocks[4 * a + 2 * half + 1, rows, :].astype(F32)
            pairs.append(
                (jnp.where(low, first, swap_halves(second)), jnp.where(low, swap_halves(first), second))
            )
        return pairs

    return load


def emit_blocks(blocks):
    def emit(block, rows, half, re, im):
        low = low_lanes()
        for a in range(8):
            blocks[4 * a + 2 * half, rows, :] = jnp.where(low, re[a], swap_halves(im[a])).astype(BF16)
            blocks[4 * a + 2 * half + 1, rows, :] = jnp.where(low, swap_halves(re[a]), im[a]).astype(BF16)

    return emit


def taps_of(position, places):
    distance = places - position
    inside = (distance > -4.0) & (distance <= 4.0)
    return jnp.where(inside, jnp.exp2(distance * distance * TAP_RATE), 0.0)


def place_index():
    place = lax.broadcasted_iota(jnp.int32, (TILE, V), 0)
    return (place // 8 + 8 * lax.rem(place, 8) - 3).astype(F32)


def grid_tile(tile, packed, weight, places):
    u_part = packed // 8192
    u_place = u_part.astype(F32) * (1.0 / OVER)
    v_place = (packed - u_part * 8192).astype(F32) * (1.0 / OVER)
    taps_u = taps_of(u_place, places).astype(BF16)
    taps_v = taps_of(v_place, places).astype(BF16).astype(F32)
    partial = lax.dot_general(tile, taps_u, (((0,), (0,)), ((), ())), preferred_element_type=F32)
    real = jnp.sum(partial[0:64] * taps_v, axis=0, keepdims=True) * weight
    imag = jnp.sum(partial[64:128] * taps_v, axis=0, keepdims=True) * -weight
    spread = jnp.concatenate([taps_v * real, taps_v * imag], axis=0).astype(BF16)
    return lax.dot_general(taps_u, spread, (((1,), (1,)), ((), ())), preferred_element_type=F32).astype(BF16)


def exchange_start(source, target, send, recv, me):
    def step(offset, carry):
        peer = lax.rem(me + offset, ROWS)
        pltpu.make_async_remote_copy(
            source.at[peer], target.at[me], send.at[peer], recv.at[me], device_id={"row": peer}, device_id_type=MESH
        ).start()
        return carry

    lax.fori_loop(1, ROWS, step, 0)


def exchange_wait(source, target, send, recv, me):
    def step(offset, carry):
        peer = lax.rem(me + offset, ROWS)
        copy = pltpu.make_async_remote_copy(
            source.at[peer], target.at[peer], send.at[peer], recv.at[peer], device_id={"row": peer}, device_id_type=MESH
        )
        copy.wait_send()
        copy.wait_recv()
        return carry

    lax.fori_loop(1, ROWS, step, 0)


def greet(axis, size, me, barrier):
    def step(offset, carry):
        pl.semaphore_signal(
            barrier, inc=1, device_id={axis: lax.rem(me + offset, size)}, device_id_type=MESH
        )
        return carry

    lax.fori_loop(1, size, step, 0)


def first_kernel(
    w_ref, image, packed, weight, table, twiddle, got, got_packed, got_weight, stacked, blocks, send, recv
):
    me = lax.axis_index("row")
    barrier = pltpu.get_barrier_semaphore()
    greet("row", ROWS, me, barrier)
    w = w_ref[0]

    def load(block, rows, half):
        pairs = []
        for a in range(8):
            col = 256 * a + 128 * half
            cosine, sine = chunk_screen(w, me * 64 + block * 16, col)
            real, imag = image[0, rows, col : col + 128], image[1, rows, col : col + 128]
            pairs.append((real * cosine + imag * sine, real * sine - imag * cosine))
        return pairs

    pl.semaphore_wait(barrier, ROWS - 1)
    exchange_start(packed, got_packed, send.at[0], recv.at[0], me)
    exchange_start(weight, got_weight, send.at[1], recv.at[1], me)
    got_packed[me] = packed[me]
    got_weight[me] = weight[me]
    spread_out(load, twiddle, stacked)
    turn_blocks(stacked, table, blocks)
    exchange_start(blocks, got, send.at[2], recv.at[2], me)
    got[me] = blocks[me]
    exchange_wait(packed, got_packed, send.at[0], recv.at[0], me)
    exchange_wait(weight, got_weight, send.at[1], recv.at[1], me)
    exchange_wait(blocks, got, send.at[2], recv.at[2], me)


def second_kernel(
    owner, got, packed, weight, table, twiddle, out, stacked, tiles, gridded, middle, slots, seen
):
    me = lax.axis_index("row")
    for place in range(ROWS):
        seen[place] = 0

    def rank(item, carry):
        name = owner[me * ROWS + item]
        before = seen[name]
        slots[item] = name * 2 + before
        seen[name] = before + 1
        return carry

    lax.fori_loop(0, ROWS, rank, 0)
    spread_out(load_received(got), twiddle, stacked)
    turn_blocks(stacked, table, tiles)
    places = place_index()

    def step(item, carry):
        slot = slots[item]
        name, second = slot // 2, lax.rem(slot, 2)
        gridded[item] = grid_tile(
            tiles[item], packed[name, pl.ds(second, 1), :], weight[name, pl.ds(second, 1), :], places
        )
        return carry

    lax.fori_loop(0, ROWS, step, 0, unroll=2)
    gather_blocks(gridded, table, twiddle, middle)
    gather_last(middle, emit_blocks(out))


def third_kernel(
    w_ref, blocks, table, twiddle, out, got, middle, screen, terms, others, send, recv, plane_send, plane_recv
):
    me = lax.axis_index("row")
    plane = lax.axis_index("plane")
    barrier = pltpu.get_barrier_semaphore()
    greet("row", ROWS, me, barrier)
    greet("plane", PLANES, plane, barrier)
    pl.semaphore_wait(barrier, ROWS + PLANES - 2)
    exchange_start(blocks, got, send, recv, me)
    got[me] = blocks[me]
    w = w_ref[0]

    def prepare(block, carry):
        rows = pl.ds(pl.multiple_of(block * 16, 16), 16)
        for piece in range(16):
            lanes = slice(128 * piece, 128 * piece + 128)
            cosine, sine = chunk_screen(w, me * 64 + block * 16, 128 * piece)
            screen[0, rows, lanes] = cosine
            screen[1, rows, lanes] = sine
        return carry

    lax.fori_loop(0, 4, prepare, 0)
    exchange_wait(blocks, got, send, recv, me)
    gather_blocks(got, table, twiddle, middle)

    def emit(block, rows, half, re, im):
        for a in range(8):
            lanes = slice(128 * half, 128 * half + 128)
            full = slice(256 * a + 128 * half, 256 * a + 128 * half + 128)
            cosine, sine = screen[0, rows, full], screen[1, rows, full]
            terms[a, 0, rows, lanes] = (re[a] * cosine - im[a] * sine).astype(BF16)
            terms[a, 1, rows, lanes] = (re[a] * sine + im[a] * cosine).astype(BF16)

    gather_last(middle, emit)
    for offset in range(1, PLANES):
        peer = lax.rem(plane + offset, PLANES)
        pltpu.make_async_remote_copy(
            terms.at[peer],
            others.at[plane],
            plane_send.at[peer],
            plane_recv.at[plane],
            device_id={"plane": peer},
            device_id_type=MESH,
        ).start()
    out[...] = terms[plane].astype(F32)
    for offset in range(1, PLANES):
        peer = lax.rem(plane + offset, PLANES)
        copy = pltpu.make_async_remote_copy(
            terms.at[peer],
            others.at[peer],
            plane_send.at[peer],
            plane_recv.at[peer],
            device_id={"plane": peer},
            device_id_type=MESH,
        )
        copy.wait_send()
        copy.wait_recv()
        out[...] += others[peer].astype(F32)


def local(image, w_planes, owner, positions, weights, counts):
    table, twiddle = host_tables()
    table, twiddle = jnp.asarray(table), jnp.asarray(twiddle)
    vmem = pl.BlockSpec(memory_space=pltpu.VMEM)
    smem = pl.BlockSpec(memory_space=pltpu.SMEM)
    packed = (positions[0, 0] * 8192 + positions[0, 1]).reshape(ROWS, 2, V)
    usable = jnp.arange(V, dtype=jnp.int32)[None, :] < counts[0][:, None]
    weight = jnp.where(usable, weights[0], 0.0).reshape(ROWS, 2, V)
    dma = pltpu.SemaphoreType.DMA
    block_shape = jax.ShapeDtypeStruct((ROWS, TILE, 128), BF16)
    got, packed, weight = pl.pallas_call(
        first_kernel,
        out_shape=(
            block_shape,
            jax.ShapeDtypeStruct((ROWS, 2, V), jnp.int32),
            jax.ShapeDtypeStruct((ROWS, 2, V), F32),
        ),
        in_specs=[smem] + [vmem] * 5,
        out_specs=(vmem, vmem, vmem),
        scratch_shapes=[
            pltpu.VMEM((8, 64, 512), BF16),
            pltpu.VMEM((ROWS, TILE, 128), BF16),
            dma((3, ROWS)),
            dma((3, ROWS)),
        ],
        compiler_params=pltpu.CompilerParams(collective_id=0, has_side_effects=True),
        name="first",
    )(w_planes, image, packed, weight, table, twiddle)
    blocks = pl.pallas_call(
        second_kernel,
        out_shape=block_shape,
        in_specs=[smem] + [vmem] * 5,
        out_specs=vmem,
        scratch_shapes=[
            pltpu.VMEM((8, 64, 512), BF16),
            pltpu.VMEM((ROWS, TILE, 128), BF16),
            pltpu.VMEM((ROWS, TILE, 128), BF16),
            pltpu.VMEM((8, 64, 512), F32),
            pltpu.SMEM((ROWS,), jnp.int32),
            pltpu.SMEM((ROWS,), jnp.int32),
        ],
        name="second",
    )(owner.reshape(-1), got, packed, weight, table, twiddle)
    return pl.pallas_call(
        third_kernel,
        out_shape=jax.ShapeDtypeStruct((2, 64, 256), F32),
        in_specs=[smem] + [vmem] * 3,
        out_specs=vmem,
        scratch_shapes=[
            pltpu.VMEM((ROWS, TILE, 128), BF16),
            pltpu.VMEM((8, 64, 512), F32),
            pltpu.VMEM((2, 64, EXTENT), F32),
            pltpu.VMEM((PLANES, 2, 64, 256), BF16),
            pltpu.VMEM((PLANES, 2, 64, 256), BF16),
            dma((ROWS,)),
            dma((ROWS,)),
            dma((PLANES,)),
            dma((PLANES,)),
        ],
        compiler_params=pltpu.CompilerParams(collective_id=1, has_side_effects=True),
        name="third",
    )(w_planes, blocks, table, twiddle)


def solution(mesh):
    in_specs = (
        P(None, "row", None),
        P("plane"),
        P("plane", None, None),
        P("plane", None, "row", None),
        P("plane", "row", None),
        P("plane", "row"),
    )
    out_specs = P(None, "row", "plane")
    return jax.shard_map(local, mesh=mesh, in_specs=in_specs, out_specs=out_specs, check_vma=False)
```

profile of v0, /device:TPU:1, one launch (start us, length us, event | category | flops | bytes accessed | tf_op | source)
XLA Modules:
  0.0 78.0 jit_solution(16631587357570983657)
XLA Ops:
  0.7 0.0 copy-start.1
  0.7 0.5 broadcast.12
  1.2 0.1 copy-done.1
  1.3 0.7 reduce.3
  2.0 0.1 lt.17
  2.1 0.9 %slice_add_fusion = s32[1,1,64,256]{3,2,1,0:T(8,128)S(1)} fusion(s32[1,2,64,256]{3,2,1,0:T(8,128)} %param.11), kind=kLoop, calls=%fused_computation.1 | loop fusion | flops 32768 | bytes 196608 | tf_op jit(solution)/shard_map/add | solution.py:366
  3.0 0.0 copy-start
  3.0 0.7 add.8.packed
  3.6 0.2 copy-done
  3.9 0.7 compare_select_fusion.weight
  4.6 29.1 %first.1 = (bf16[32,64,128]{2,1,0:T(8,128)(2,1)}, s32[32,2,256]{2,1,0:T(2,128)}, f32[32,2,256]{2,1,0:T(2,128)}) custom-call(f32[1]{0:T(128)S(6)} %copy.10.w_ref, f32[2,64,2048]{2,1,0:T(8,128)} %image.1, s32[32,2,256]{2,1,0:T(2,128)} %add.8.packed, f32[32,2,256]{2,1,0:T(2,128)} %compare_select_fusion.weight, bf16[512,512]{1,0:T(8,128)(2,1)} %constant.8.clone.table, ...), custom_call_target="tpu_custom_call" | custom-call | tf_op jit(solution)/shard_map/first/pallas_call | solution.py:371
  33.7 11.2 %second.1.blocks = bf16[32,64,128]{2,1,0:T(8,128)(2,1)} custom-call(s32[1024]{0:T(1024)} %bitcast.3, bf16[32,64,128]{2,1,0:T(8,128)(2,1)} %get-tuple-element.8.got, s32[32,2,256]{2,1,0:T(2,128)} %get-tuple-element.9.packed, f32[32,2,256]{2,1,0:T(2,128)} %get-tuple-element.10.weight, bf16[512,512]{1,0:T(8,128)(2,1)} %constant.8.clone.table, ...), custom_call_target="tpu_custom_call" | custom-call | tf_op jit(solution)/shard_map/second/pallas_call | solution.py:389
  44.9 31.5 %third.1 = f32[2,64,256]{2,1,0:T(8,128)} custom-call(f32[1]{0:T(128)S(6)} %copy.10.w_ref, bf16[32,64,128]{2,1,0:T(8,128)(2,1)} %second.1.blocks, bf16[512,512]{1,0:T(8,128)(2,1)} %constant.8.clone.table, f32[2,8,256]{2,1,0:T(8,128)} %constant.9.clone.twiddle), custom_call_target="tpu_custom_call" | custom-call | tf_op jit(solution)/shard_map/third/pallas_call | solution.py:404
  76.4 1.6 %copy.11 = f32[2,64,256]{2,1,0:T(8,128)} copy(f32[2,64,256]{2,1,0:T(8,128)} %third.1) | data formatting | bytes 262144
  (1 shorter events, 0.0 us)
Async XLA Ops:
  0.7 0.7 copy-start.1
  3.0 0.8 %copy-start = (f32[1,64,256]{2,1,0:T(8,128)S(1)}, f32[1,64,256]{2,1,0:T(8,128)}, u32[]{:S(2)}) copy-start(f32[1,64,256]{2,1,0:T(8,128)} %param.12) | copy-start | bytes 196612
where the time goes:
time: 78.3 us; the launch traced here: 78 us
  Pallas kernels  71.8 us (92%)
  local copies, waits for them, and re-layouts  3.18 us (4%)
  other arithmetic  2.29 us (3%)
    pallas_call x1, Pallas kernels, local(): pl.pallas_call(third_kernel, out_shape=jax.ShapeDtypeStruct((2, 64, 256),...  31.5 us
    pallas_call x1, Pallas kernels, local(): pl.pallas_call(first_kernel, out_shape=(block_shape, jax.ShapeDtypeStruct...  29.1 us
    pallas_call x1, Pallas kernels, local(): pl.pallas_call(second_kernel, out_shape=block_shape, in_specs=[smem] + [v...  11.2 us
    unnamed x6, local copies, waits for them, and re-layouts  2.38 us

commit v1 on v0

v1 whole, which is shorter than its diff:
```python
import functools

import jax
import jax.numpy as jnp
import ml_dtypes
import numpy as np
from jax import lax
from jax.experimental import pallas as pl
from jax.experimental.pallas import tpu as pltpu
from jax.sharding import PartitionSpec as P

TILE = 64
S = 8
OVER = 128
V = 256
FIELD_SPAN = 0.7
EXTENT = 2048
ROWS = 32
PLANES = 8
SCALE = 1.0 / 2048.0
TAP_RATE = -4.0 * 1.4426950408889634
MESH = pl.DeviceIdType.MESH
F32 = jnp.float32
BF16 = jnp.bfloat16
ROOT = 0.7071067811865476
SIN_POLY = (6.283184916495429, -41.34158923268831, 81.59994332977428, -76.61447253115396, 41.342882354135696, -12.471243534350362)
COS_POLY = (0.9999999890590228, -19.739204499453827, 64.9391174598908, -85.45013953079768, 60.16763095026347, -25.967599245923736, 6.52865815775625)


def host_tables():
    index = np.arange(256)
    angle = 2.0 * np.pi / 256.0 * (index[:, None] * index[None, :] % 256)
    cosine, sine = np.cos(angle), np.sin(angle)
    table = np.block([[cosine, sine], [-sine, cosine]]).astype(ml_dtypes.bfloat16)
    turn = 2.0 * np.pi / 2048.0 * (np.arange(8)[:, None] * index[None, :])
    return table, np.stack([np.cos(turn), np.sin(turn)]).astype(np.float32)


def dft4(re, im):
    ar, ai, br, bi = re[0] + re[2], im[0] + im[2], re[0] - re[2], im[0] - im[2]
    cr, ci, dr, di = re[1] + re[3], im[1] + im[3], re[1] - re[3], im[1] - im[3]
    return [ar + cr, br - di, ar - cr, br + di], [ai + ci, bi + dr, ai - ci, bi - dr]


def dft8(re, im):
    er, ei = dft4(re[0::2], im[0::2])
    od, oi = dft4(re[1::2], im[1::2])
    tr = [od[0], (od[1] - oi[1]) * ROOT, -oi[2], (od[3] + oi[3]) * -ROOT]
    ti = [oi[0], (od[1] + oi[1]) * ROOT, od[2], (od[3] - oi[3]) * ROOT]
    return [er[k] + tr[k] for k in range(4)] + [er[k] - tr[k] for k in range(4)], [
        ei[k] + ti[k] for k in range(4)
    ] + [ei[k] - ti[k] for k in range(4)]


def swap_halves(value):
    return pltpu.roll(value, 64, 1)


def screen_of(turns):
    part = turns - jnp.round(turns)
    square = part * part
    sine = jnp.full_like(part, SIN_POLY[-1])
    for term in SIN_POLY[-2::-1]:
        sine = sine * square + term
    cosine = jnp.full_like(part, COS_POLY[-1])
    for term in COS_POLY[-2::-1]:
        cosine = cosine * square + term
    return cosine * SCALE, sine * part * SCALE


def chunk_screen(w, row_start, col_start):
    spacing = FIELD_SPAN / EXTENT
    rows = lax.broadcasted_iota(jnp.int32, (16, 128), 0) + (row_start - EXTENT // 2)
    cols = lax.broadcasted_iota(jnp.int32, (16, 128), 1) + (col_start - EXTENT // 2)
    rows = rows.astype(F32) * spacing
    cols = cols.astype(F32) * spacing
    elevation = jnp.sqrt(1.0 - rows * rows - cols * cols) - 1.0
    return screen_of(w * elevation)


def spread_block(load, block, twiddle, stacked):
    rows = pl.ds(pl.multiple_of(block * 16, 16), 16)
    for half in range(2):
        pairs = load(block, rows, half)
        re, im = dft8([pair[0] for pair in pairs], [pair[1] for pair in pairs])
        lanes = slice(128 * half, 128 * half + 128)
        other = slice(256 + 128 * half, 384 + 128 * half)
        for q in range(8):
            if q == 0:
                real, imag = re[0], im[0]
            else:
                cosine, sine = twiddle[0, q : q + 1, lanes], twiddle[1, q : q + 1, lanes]
                real, imag = re[q] * cosine - im[q] * sine, re[q] * sine + im[q] * cosine
            stacked[q, rows, lanes] = real.astype(BF16)
            stacked[q, rows, other] = imag.astype(BF16)


def turn_blocks(stacked, table, blocks):
    matrix = table[...]
    for pair in range(4):
        left = stacked[2 * pair : 2 * pair + 2].reshape(128, 512)
        out = jnp.dot(left, matrix, preferred_element_type=F32)
        for half in range(2):
            real, imag = slice(128 * half, 128 * half + 128), slice(256 + 128 * half, 384 + 128 * half)
            turned = []
            for item in range(2):
                rows = slice(64 * item, 64 * item + 64)
                square = jnp.concatenate([out[rows, real], out[rows, imag]], axis=0)
                turned.append(jnp.transpose(square).reshape(16, 8, 128))
            both = jnp.concatenate(turned, axis=1).astype(BF16)
            blocks[16 * half : 16 * half + 16, 16 * pair : 16 * pair + 16, :] = both


def gather_pair(pair, blocks, table, twiddle, middle):
    matrix = table[...]
    rows = blocks[:, pl.ds(pl.multiple_of(16 * pair, 16), 16), :].astype(F32)
    for item in range(2):
        q = 2 * pair + item
        flat = rows[:, 8 * item : 8 * item + 8, :].reshape(256, 128)
        low = jnp.transpose(flat[0:128]).astype(BF16)
        high = jnp.transpose(flat[128:256]).astype(BF16)
        left = jnp.concatenate([low[0:64], high[0:64], low[64:128], high[64:128]], axis=1)
        out = jnp.dot(left, matrix, preferred_element_type=F32)
        real, imag = out[:, 0:256], out[:, 256:512]
        cosine, sine = twiddle[0, pl.ds(q, 1), :], twiddle[1, pl.ds(q, 1), :]
        middle[q, :, 0:256] = real * cosine - imag * sine
        middle[q, :, 256:512] = real * sine + imag * cosine


def last_block(block, middle, emit):
    rows = pl.ds(pl.multiple_of(block * 16, 16), 16)
    for half in range(2):
        lanes = slice(128 * half, 128 * half + 128)
        other = slice(256 + 128 * half, 384 + 128 * half)
        re, im = dft8([middle[q, rows, lanes] for q in range(8)], [middle[q, rows, other] for q in range(8)])
        emit(block, rows, half, re, im)


def low_lanes():
    return lax.broadcasted_iota(jnp.int32, (16, 128), 1) < 64


def load_received(blocks):
    def load(block, rows, half):
        low = low_lanes()
        pairs = []
        for a in range(8):
            first = blocks[4 * a + 2 * half, rows, :].astype(F32)
            second = blocks[4 * a + 2 * half + 1, rows, :].astype(F32)
            pairs.append(
                (jnp.where(low, first, swap_halves(second)), jnp.where(low, swap_halves(first), second))
            )
        return pairs

    return load


def emit_blocks(blocks):
    def emit(block, rows, half, re, im):
        low = low_lanes()
        for a in range(8):
            blocks[4 * a + 2 * half, rows, :] = jnp.where(low, re[a], swap_halves(im[a])).astype(BF16)
            blocks[4 * a + 2 * half + 1, rows, :] = jnp.where(low, swap_halves(re[a]), im[a]).astype(BF16)

    return emit


def taps_of(position, places):
    distance = places - position
    inside = (distance > -4.0) & (distance <= 4.0)
    return jnp.where(inside, jnp.exp2(distance * distance * TAP_RATE), 0.0)


def place_index():
    place = lax.broadcasted_iota(jnp.int32, (TILE, V), 0)
    return (place // 8 + 8 * lax.rem(place, 8) - 3).astype(F32)


def grid_tile(tile, taps_u, taps_v, weight):
    partial = lax.dot_general(tile, taps_u, (((0,), (0,)), ((), ())), preferred_element_type=F32)
    real = jnp.sum(partial[0:64] * taps_v, axis=0, keepdims=True) * weight
    imag = jnp.sum(partial[64:128] * taps_v, axis=0, keepdims=True) * -weight
    spread = jnp.concatenate([taps_v * real, taps_v * imag], axis=0).astype(BF16)
    return lax.dot_general(taps_u, spread, (((1,), (1,)), ((), ())), preferred_element_type=F32).astype(BF16)


def chunk_rows(chunk):
    return pl.ds(pl.multiple_of(chunk * 16, 16), 16)


def send_all(axis, size, me, source, target, send, recv):
    def step(offset, carry):
        peer = lax.rem(me + offset, size)
        pltpu.make_async_remote_copy(
            source(peer), target, send, recv, device_id={axis: peer}, device_id_type=MESH
        ).start()
        return carry

    lax.fori_loop(1, size, step, 0)


def wait_recv(view, recv):
    pltpu.make_async_copy(view, view, recv).wait()


def greet(axis, size, me, barrier):
    def step(offset, carry):
        pl.semaphore_signal(
            barrier, inc=1, device_id={axis: lax.rem(me + offset, size)}, device_id_type=MESH
        )
        return carry

    lax.fori_loop(1, size, step, 0)


def whole_kernel(
    w_ref,
    owner,
    counts,
    image_in,
    positions_in,
    weights_in,
    table_in,
    twiddle_in,
    others,
    image,
    positions,
    weights,
    table,
    twiddle,
    packed,
    kept,
    got_packed,
    got_kept,
    stacked,
    blocks,
    got,
    tiles,
    gridded,
    back,
    got_back,
    middle,
    screen,
    terms,
    all_taps,
    tile_weight,
    local_sem,
    vis_send,
    vis_recv,
    out_send,
    out_recv,
    back_send,
    back_recv,
    term_send,
    term_recv,
):
    me = lax.axis_index("row")
    plane = lax.axis_index("plane")
    barrier = pltpu.get_barrier_semaphore()
    greet("row", ROWS, me, barrier)
    greet("plane", PLANES, plane, barrier)
    loads = [
        pltpu.make_async_copy(source, target, local_sem.at[index])
        for index, (source, target) in enumerate(
            (
                (image_in, image),
                (twiddle_in, twiddle),
                (positions_in, positions),
                (weights_in, weights),
                (table_in, table),
            )
        )
    ]
    for copy in loads:
        copy.start()
    w = w_ref[0]

    def load(block, rows, half):
        pairs = []
        for a in range(8):
            col = 256 * a + 128 * half
            cosine, sine = screen[0, rows, col : col + 128], screen[1, rows, col : col + 128]
            real, imag = image[0, rows, col : col + 128], image[1, rows, col : col + 128]
            pairs.append((real * cosine + imag * sine, real * sine - imag * cosine))
        return pairs

    def prepare(block, carry):
        rows = chunk_rows(block)
        for piece in range(16):
            lanes = slice(128 * piece, 128 * piece + 128)
            cosine, sine = chunk_screen(w, me * 64 + block * 16, 128 * piece)
            screen[0, rows, lanes] = cosine
            screen[1, rows, lanes] = sine
        return carry

    lax.fori_loop(0, 4, prepare, 0)
    for copy in loads[0:4]:
        copy.wait()
    place_of = lax.broadcasted_iota(jnp.int32, (1, V), 1)
    for peer in range(ROWS):
        pair = slice(2 * peer, 2 * peer + 2)
        packed[peer] = positions[0, 0, pair, :] * 8192 + positions[0, 1, pair, :]
        for item in range(2):
            slot = 2 * peer + item
            kept[peer, item : item + 1, :] = jnp.where(
                place_of < counts[0, slot], weights[0, slot : slot + 1, :], 0.0
            )

    def first_spread(block, carry):
        spread_block(load, block, twiddle, stacked)
        return carry

    lax.fori_loop(0, 4, first_spread, 0)
    loads[4].wait()
    turn_blocks(stacked, table, blocks)
    pl.semaphore_wait(barrier, ROWS + PLANES - 2)
    send_all("row", ROWS, me, lambda peer: packed.at[peer], got_packed.at[me], vis_send.at[0], vis_recv.at[0])
    send_all("row", ROWS, me, lambda peer: kept.at[peer], got_kept.at[me], vis_send.at[1], vis_recv.at[1])

    def send_chunk(chunk, carry):
        rows = chunk_rows(chunk)
        send_all(
            "row", ROWS, me, lambda peer: blocks.at[peer, rows], got.at[me, rows], out_send.at[chunk], out_recv.at[chunk]
        )
        return carry

    lax.fori_loop(0, 4, send_chunk, 0)
    got_packed[me] = packed[me]
    got_kept[me] = kept[me]
    got[me] = blocks[me]
    places = place_index()
    most = pl.ds(0, ROWS - 1)
    wait_recv(got_packed.at[most], vis_recv.at[0])
    wait_recv(got_kept.at[most], vis_recv.at[1])

    def tap_step(item, carry):
        name = owner[me * ROWS + item]

        def count(other, total):
            return total + jnp.where((owner[me * ROWS + other] == name) & (other < item), 1, 0)

        second = lax.fori_loop(0, ROWS, count, 0, unroll=True) > 0
        both, pair = got_packed[name], got_kept[name]
        place = jnp.where(second, both[1:2], both[0:1])
        u_part = place // 8192
        all_taps[item, 0] = taps_of(u_part.astype(F32) * (1.0 / OVER), places).astype(BF16)
        all_taps[item, 1] = taps_of((place - u_part * 8192).astype(F32) * (1.0 / OVER), places).astype(BF16)
        tile_weight[item] = jnp.where(second, pair[1:2], pair[0:1])
        return carry

    lax.fori_loop(0, ROWS, tap_step, 0)
    load_got = load_received(got)

    def second_spread(chunk, carry):
        wait_recv(got.at[most, chunk_rows(chunk)], out_recv.at[chunk])
        spread_block(load_got, chunk, twiddle, stacked)
        return carry

    lax.fori_loop(0, 4, second_spread, 0)
    turn_blocks(stacked, table, tiles)

    def grid_step(item, carry):
        gridded[item] = grid_tile(
            tiles[item], all_taps[item, 0], all_taps[item, 1].astype(F32), tile_weight[item]
        )
        return carry

    lax.fori_loop(0, ROWS, grid_step, 0, unroll=2)

    def gather_step(pair, carry):
        gather_pair(pair, gridded, table, twiddle, middle)
        return carry

    lax.fori_loop(0, 4, gather_step, 0)
    emit_back = emit_blocks(back)

    def back_chunk(chunk, carry):
        last_block(chunk, middle, emit_back)
        rows = chunk_rows(chunk)
        send_all(
            "row",
            ROWS,
            me,
            lambda peer: back.at[peer, rows],
            got_back.at[me, rows],
            back_send.at[chunk],
            back_recv.at[chunk],
        )
        return carry

    lax.fori_loop(0, 4, back_chunk, 0)
    got_back[me] = back[me]

    def final_gather(chunk, carry):
        wait_recv(got_back.at[most, chunk_rows(chunk)], back_recv.at[chunk])
        gather_pair(chunk, got_back, table, twiddle, middle)
        return carry

    lax.fori_loop(0, 4, final_gather, 0)

    def emit(block, rows, half, re, im):
        for a in range(8):
            lanes = slice(128 * half, 128 * half + 128)
            full = slice(256 * a + 128 * half, 256 * a + 128 * half + 128)
            cosine, sine = screen[0, rows, full], screen[1, rows, full]
            terms[a, 0, rows, lanes] = (re[a] * cosine - im[a] * sine).astype(BF16)
            terms[a, 1, rows, lanes] = (re[a] * sine + im[a] * cosine).astype(BF16)

    def term_chunk(chunk, carry):
        last_block(chunk, middle, emit)
        rows = chunk_rows(chunk)
        send_all(
            "plane", PLANES, plane, lambda peer: terms.at[peer, :, rows], others.at[plane, :, rows], term_send, term_recv
        )
        return carry

    lax.fori_loop(0, 4, term_chunk, 0)
    mine = pltpu.make_async_copy(terms.at[plane], others.at[plane], local_sem.at[0])
    mine.start()
    wait_recv(packed.at[most], vis_send.at[0])
    wait_recv(kept.at[most], vis_send.at[1])
    for chunk in range(4):
        wait_recv(blocks.at[most, chunk_rows(chunk)], out_send.at[chunk])
        wait_recv(back.at[most, chunk_rows(chunk)], back_send.at[chunk])
    mine.wait()
    rest = pl.ds(0, PLANES - 1)
    wait_recv(terms.at[rest], term_send)
    wait_recv(others.at[rest], term_recv)


def local(image, w_planes, owner, positions, weights, counts):
    table, twiddle = host_tables()
    smem = pl.BlockSpec(memory_space=pltpu.SMEM)
    anywhere = pl.BlockSpec(memory_space=pl.ANY)
    dma = pltpu.SemaphoreType.DMA
    block = pltpu.VMEM((ROWS, TILE, 128), BF16)
    others = pl.pallas_call(
        whole_kernel,
        out_shape=jax.ShapeDtypeStruct((PLANES, 2, 64, 256), BF16),
        in_specs=[smem] * 3 + [anywhere] * 5,
        out_specs=anywhere,
        scratch_shapes=[
            pltpu.VMEM((2, 64, EXTENT), F32),
            pltpu.VMEM((1, 2, 64, V), jnp.int32),
            pltpu.VMEM((1, 64, V), F32),
            pltpu.VMEM((512, 512), BF16),
            pltpu.VMEM((2, 8, 256), F32),
            pltpu.VMEM((ROWS, 2, V), jnp.int32),
            pltpu.VMEM((ROWS, 2, V), F32),
            pltpu.VMEM((ROWS, 2, V), jnp.int32),
            pltpu.VMEM((ROWS, 2, V), F32),
            pltpu.VMEM((8, 64, 512), BF16),
            block,
            block,
            block,
            block,
            block,
            block,
            pltpu.VMEM((8, 64, 512), F32),
            pltpu.VMEM((2, 64, EXTENT), F32),
            pltpu.VMEM((PLANES, 2, 64, 256), BF16),
            pltpu.VMEM((ROWS, 2, TILE, V), BF16),
            pltpu.VMEM((ROWS, 1, V), F32),
            dma((5,)),
            dma((2,)),
            dma((2,)),
            dma((4,)),
            dma((4,)),
            dma((4,)),
            dma((4,)),
            dma,
            dma,
        ],
        compiler_params=pltpu.CompilerParams(collective_id=0, has_side_effects=True),
        name="whole",
    )(
        w_planes,
        owner.reshape(-1),
        counts,
        image,
        positions,
        weights,
        jnp.asarray(table),
        jnp.asarray(twiddle),
    )
    return jnp.sum(others.astype(F32), axis=0)


def solution(mesh):
    in_specs = (
        P(None, "row", None),
        P("plane"),
        P("plane", None, None),
        P("plane", None, "row", None),
        P("plane", "row", None),
        P("plane", "row"),
    )
    out_specs = P(None, "row", "plane")
    return jax.shard_map(local, mesh=mesh, in_specs=in_specs, out_specs=out_specs, check_vma=False)
```

time: 78.3 us -> 64 us (0.82)
  Pallas kernels: 71.8 us -> 61.4 us
  local copies, waits for them, and re-layouts: 3.18 us -> 0 us
    pallas_call x3 -> x1, Pallas kernels: 71.8 us -> 61.4 us  [local(): pl.pallas_call(whole_kernel, out_shape=jax.ShapeDtypeStruct((PLANES, 2, 6...]
    unnamed x6 -> x0, local copies, waits for them, and re-layouts: 2.38 us -> none
    reduce_sum x0 -> x1, other arithmetic: none -> 1.78 us  [local(): return jnp.sum(others.astype(F32), axis=0)]
    add x1 -> x0, other arithmetic: 0.89 us -> none  [local(): packed = (positions[0, 0] * 8192 + positions[0, 1]).reshape(ROWS, 2, V)]
where the time goes in v1:
time: 64 us; the launch traced here: 63.8 us
  Pallas kernels  61.4 us (96%)
  other arithmetic  1.78 us (3%)
  between operations  0.66 us (1%)
    pallas_call x1, Pallas kernels, local(): pl.pallas_call(whole_kernel, out_shape=jax.ShapeDtypeStruct((PLANES, 2, 6...  61.4 us
    reduce_sum x1, other arithmetic, local(): return jnp.sum(others.astype(F32), axis=0)  1.78 us

profile of v1, /device:TPU:1, one launch (start us, length us, event | category | flops | bytes accessed | tf_op | source)
XLA Modules:
  0.0 63.8 jit_solution(16528854784477400357)
XLA Ops:
  0.7 61.4 %whole.1 = bf16[8,2,64,256]{3,2,1,0:T(8,128)(2,1)} custom-call(f32[1]{0:T(128)S(6)} %copy.9.w_ref, s32[1024]{0:T(1024)} %bitcast.1, s32[1,64]{1,0:T(1,128)} %counts.1, f32[2,64,2048]{2,1,0:T(8,128)} %image_in.1, s32[1,2,64,256]{3,2,1,0:T(8,128)} %positions_in.1, f32[1,64,256]{2,1,0:T(8,128)} %weights_in.1, bf16[512,512]{1,0:T(8,128)(2,1)} %constant.6.clone.table_in, ...), custom_call_target="tpu_custom_call" | custom-call | tf_op jit(solution)/shard_map/whole/pallas_call | solution.py:437
  62.0 1.8 %convert_reduce_fusion = f32[2,64,256]{2,1,0:T(8,128)} fusion(bf16[8,2,64,256]{3,2,1,0:T(8,128)(2,1)} %whole.1), kind=kLoop, calls=%fused_computation | loop fusion | flops 491520 | bytes 655360 | tf_op jit(solution)/shard_map/reduce_sum | solution.py:486

commit v2 on v1

--- a/solution.py
+++ b/solution.py
@@ -127,6 +127,29 @@
         middle[q, :, 256:512] = real * sine + imag * cosine
 
 
+def gather_chunk(chunk, blocks, table, twiddle, middle):
+    values = blocks[chunk].astype(F32)
+    left = []
+    for item in range(2):
+        flat = values[:, 8 * item : 8 * item + 8, :].reshape(256, 128)
+        low = jnp.transpose(flat[0:128]).reshape(4, 2, 16, 128)
+        high = jnp.transpose(flat[128:256]).reshape(4, 2, 16, 128)
+        parts = [low[:, 0], high[:, 0], low[:, 1], high[:, 1]]
+        left.append(jnp.concatenate([part.reshape(64, 128) for part in parts], axis=1))
+    out = jnp.dot(jnp.concatenate(left, axis=0).astype(BF16), table[...], preferred_element_type=F32)
+    rows = chunk_rows(chunk)
+    for item in range(2):
+        for place in range(4):
+            q = 2 * place + item
+            piece = out[64 * item + 16 * place : 64 * item + 16 * place + 16]
+            real, imag = piece[:, 0:256], piece[:, 256:512]
+            if q:
+                cosine, sine = twiddle[0, q : q + 1, :], twiddle[1, q : q + 1, :]
+                real, imag = real * cosine - imag * sine, real * sine + imag * cosine
+            middle[q, rows, 0:256] = real
+            middle[q, rows, 256:512] = imag
+
+
 def last_block(block, middle, emit):
     rows = pl.ds(pl.multiple_of(block * 16, 16), 16)
     for half in range(2):
@@ -155,14 +178,28 @@
     return load
 
 
-def emit_blocks(blocks):
+def emit_fields(fields):
     def emit(block, rows, half, re, im):
-        low = low_lanes()
         for a in range(8):
-            blocks[4 * a + 2 * half, rows, :] = jnp.where(low, re[a], swap_halves(im[a])).astype(BF16)
-            blocks[4 * a + 2 * half + 1, rows, :] = jnp.where(low, swap_halves(re[a]), im[a]).astype(BF16)
+            fields[2 * a + half, 0, rows, :] = re[a]
+            fields[2 * a + half, 1, rows, :] = im[a]
 
     return emit
+
+
+def shuffle_fields(fields, back):
+    lane = lax.broadcasted_iota(jnp.int32, (16, 128), 1)
+    for column in range(16):
+        parts = [fields[column, index % 2, 16 * (index // 2) : 16 * (index // 2) + 16, :] for index in range(8)]
+        for bit, shift in ((4, 64), (2, 32), (1, 16)):
+            low = lax.rem(lane // shift, 2) == 0
+            for index in range(8):
+                if index & bit == 0:
+                    first, second = parts[index], parts[index + bit]
+                    parts[index] = jnp.where(low, first, pltpu.roll(second, shift, 1))
+                    parts[index + bit] = jnp.where(low, pltpu.roll(first, 128 - shift, 1), second)
+        for index in range(8):
+            back[index % 4, 2 * column + index // 4] = parts[index].astype(BF16)
 
 
 def taps_of(position, places):
@@ -243,7 +280,9 @@
     screen,
     terms,
     all_taps,
-    tile_weight,
+    fields,
+    names,
+    seconds,
     local_sem,
     vis_send,
     vis_recv,
@@ -300,11 +339,11 @@
     for peer in range(ROWS):
         pair = slice(2 * peer, 2 * peer + 2)
         packed[peer] = positions[0, 0, pair, :] * 8192 + positions[0, 1, pair, :]
+        chosen = []
         for item in range(2):
             slot = 2 * peer + item
-            kept[peer, item : item + 1, :] = jnp.where(
-                place_of < counts[0, slot], weights[0, slot : slot + 1, :], 0.0
-            )
+            chosen.append(jnp.where(place_of < counts[0, slot], weights[0, slot : slot + 1, :], 0.0))
+        kept[peer] = jnp.concatenate(chosen, axis=0).astype(BF16)
 
     def first_spread(block, carry):
         spread_block(load, block, twiddle, stacked)
@@ -315,7 +354,6 @@
     turn_blocks(stacked, table, blocks)
     pl.semaphore_wait(barrier, ROWS + PLANES - 2)
     send_all("row", ROWS, me, lambda peer: packed.at[peer], got_packed.at[me], vis_send.at[0], vis_recv.at[0])
-    send_all("row", ROWS, me, lambda peer: kept.at[peer], got_kept.at[me], vis_send.at[1], vis_recv.at[1])
 
     def send_chunk(chunk, carry):
         rows = chunk_rows(chunk)
@@ -325,13 +363,13 @@
         return carry
 
     lax.fori_loop(0, 4, send_chunk, 0)
+    send_all("row", ROWS, me, lambda peer: kept.at[peer], got_kept.at[me], vis_send.at[1], vis_recv.at[1])
     got_packed[me] = packed[me]
     got_kept[me] = kept[me]
     got[me] = blocks[me]
     places = place_index()
     most = pl.ds(0, ROWS - 1)
     wait_recv(got_packed.at[most], vis_recv.at[0])
-    wait_recv(got_kept.at[most], vis_recv.at[1])
 
     def tap_step(item, carry):
         name = owner[me * ROWS + item]
@@ -340,12 +378,13 @@
             return total + jnp.where((owner[me * ROWS + other] == name) & (other < item), 1, 0)
 
         second = lax.fori_loop(0, ROWS, count, 0, unroll=True) > 0
-        both, pair = got_packed[name], got_kept[name]
+        names[item] = name
+        seconds[item] = jnp.where(second, 1, 0)
+        both = got_packed[name]
         place = jnp.where(second, both[1:2], both[0:1])
         u_part = place // 8192
         all_taps[item, 0] = taps_of(u_part.astype(F32) * (1.0 / OVER), places).astype(BF16)
         all_taps[item, 1] = taps_of((place - u_part * 8192).astype(F32) * (1.0 / OVER), places).astype(BF16)
-        tile_weight[item] = jnp.where(second, pair[1:2], pair[0:1])
         return carry
 
     lax.fori_loop(0, ROWS, tap_step, 0)
@@ -359,44 +398,32 @@
     lax.fori_loop(0, 4, second_spread, 0)
     turn_blocks(stacked, table, tiles)
 
-    def grid_step(item, carry):
-        gridded[item] = grid_tile(
-            tiles[item], all_taps[item, 0], all_taps[item, 1].astype(F32), tile_weight[item]
-        )
-        return carry
-
-    lax.fori_loop(0, ROWS, grid_step, 0, unroll=2)
-
-    def gather_step(pair, carry):
+    wait_recv(got_kept.at[most], vis_recv.at[1])
+    for item in range(ROWS):
+        pair = got_kept[names[item]].astype(F32)
+        weight = jnp.where(seconds[item] > 0, pair[1:2], pair[0:1])
+        gridded[item] = grid_tile(tiles[item], all_taps[item, 0], all_taps[item, 1].astype(F32), weight)
+    for pair in range(4):
         gather_pair(pair, gridded, table, twiddle, middle)
-        return carry
-
-    lax.fori_loop(0, 4, gather_step, 0)
-    emit_back = emit_blocks(back)
+    emit_back = emit_fields(fields)
+    for block in range(4):
+        last_block(block, middle, emit_back)
+    shuffle_fields(fields, back)
 
     def back_chunk(chunk, carry):
-        last_block(chunk, middle, emit_back)
-        rows = chunk_rows(chunk)
         send_all(
             "row",
             ROWS,
             me,
-            lambda peer: back.at[peer, rows],
-            got_back.at[me, rows],
+            lambda peer: back.at[chunk, peer],
+            got_back.at[chunk, me],
             back_send.at[chunk],
             back_recv.at[chunk],
         )
+        got_back[chunk, me] = back[chunk, me]
         return carry
 
     lax.fori_loop(0, 4, back_chunk, 0)
-    got_back[me] = back[me]
-
-    def final_gather(chunk, carry):
-        wait_recv(got_back.at[most, chunk_rows(chunk)], back_recv.at[chunk])
-        gather_pair(chunk, got_back, table, twiddle, middle)
-        return carry
-
-    lax.fori_loop(0, 4, final_gather, 0)
 
     def emit(block, rows, half, re, im):
         for a in range(8):
@@ -407,6 +434,8 @@
             terms[a, 1, rows, lanes] = (re[a] * sine + im[a] * cosine).astype(BF16)
 
     def term_chunk(chunk, carry):
+        wait_recv(got_back.at[chunk, most], back_recv.at[chunk])
+        gather_chunk(chunk, got_back, table, twiddle, middle)
         last_block(chunk, middle, emit)
         rows = chunk_rows(chunk)
         send_all(
@@ -421,7 +450,7 @@
     wait_recv(kept.at[most], vis_send.at[1])
     for chunk in range(4):
         wait_recv(blocks.at[most, chunk_rows(chunk)], out_send.at[chunk])
-        wait_recv(back.at[most, chunk_rows(chunk)], back_send.at[chunk])
+        wait_recv(back.at[chunk, most], back_send.at[chunk])
     mine.wait()
     rest = pl.ds(0, PLANES - 1)
     wait_recv(terms.at[rest], term_send)
@@ -446,21 +475,23 @@
             pltpu.VMEM((512, 512), BF16),
             pltpu.VMEM((2, 8, 256), F32),
             pltpu.VMEM((ROWS, 2, V), jnp.int32),
-            pltpu.VMEM((ROWS, 2, V), F32),
+            pltpu.VMEM((ROWS, 2, V), BF16),
             pltpu.VMEM((ROWS, 2, V), jnp.int32),
-            pltpu.VMEM((ROWS, 2, V), F32),
+            pltpu.VMEM((ROWS, 2, V), BF16),
             pltpu.VMEM((8, 64, 512), BF16),
             block,
             block,
             block,
             block,
-            block,
-            block,
+            pltpu.VMEM((4, ROWS, 16, 128), BF16),
+            pltpu.VMEM((4, ROWS, 16, 128), BF16),
             pltpu.VMEM((8, 64, 512), F32),
             pltpu.VMEM((2, 64, EXTENT), F32),
             pltpu.VMEM((PLANES, 2, 64, 256), BF16),
             pltpu.VMEM((ROWS, 2, TILE, V), BF16),
-            pltpu.VMEM((ROWS, 1, V), F32),
+            pltpu.VMEM((16, 2, 64, 128), F32),
+            pltpu.SMEM((ROWS,), jnp.int32),
+            pltpu.SMEM((ROWS,), jnp.int32),
             dma((5,)),
             dma((2,)),
             dma((2,)),

time: 64 us -> 60.4 us (0.944)
  Pallas kernels: 61.4 us -> 57.8 us
    pallas_call x1, Pallas kernels: 61.4 us -> 57.8 us  [local(): pl.pallas_call(whole_kernel, out_shape=jax.ShapeDtypeStruct((PLANES, 2, 6...]
where the time goes in v2:
time: 60.4 us; the launch traced here: 60.2 us
  Pallas kernels  57.8 us (96%)
  other arithmetic  1.78 us (3%)
  between operations  0.66 us (1%)
    pallas_call x1, Pallas kernels, local(): pl.pallas_call(whole_kernel, out_shape=jax.ShapeDtypeStruct((PLANES, 2, 6...  57.8 us
    reduce_sum x1, other arithmetic, local(): return jnp.sum(others.astype(F32), axis=0)  1.78 us

profile of v2, /device:TPU:1, one launch (start us, length us, event | category | flops | bytes accessed | tf_op | source)
XLA Modules:
  0.0 60.2 jit_solution(14822070096444622156)
XLA Ops:
  0.7 57.8 %whole.1 = bf16[8,2,64,256]{3,2,1,0:T(8,128)(2,1)} custom-call(f32[1]{0:T(128)S(6)} %copy.9.w_ref, s32[1024]{0:T(1024)} %bitcast.1, s32[1,64]{1,0:T(1,128)} %counts.1, f32[2,64,2048]{2,1,0:T(8,128)} %image_in.1, s32[1,2,64,256]{3,2,1,0:T(8,128)} %positions_in.1, f32[1,64,256]{2,1,0:T(8,128)} %weights_in.1, bf16[512,512]{1,0:T(8,128)(2,1)} %constant.6.clone.table_in, ...), custom_call_target="tpu_custom_call" | custom-call | tf_op jit(solution)/shard_map/whole/pallas_call | solution.py:466
  58.4 1.8 %convert_reduce_fusion = f32[2,64,256]{2,1,0:T(8,128)} fusion(bf16[8,2,64,256]{3,2,1,0:T(8,128)(2,1)} %whole.1), kind=kLoop, calls=%fused_computation | loop fusion | flops 491520 | bytes 655360 | tf_op jit(solution)/shard_map/reduce_sum | solution.py:517

commit v3 on v2

--- a/solution.py
+++ b/solution.py
@@ -280,6 +280,7 @@
     screen,
     terms,
     all_taps,
+    tile_weight,
     fields,
     names,
     seconds,
@@ -399,10 +400,21 @@
     turn_blocks(stacked, table, tiles)
 
     wait_recv(got_kept.at[most], vis_recv.at[1])
-    for item in range(ROWS):
-        pair = got_kept[names[item]].astype(F32)
-        weight = jnp.where(seconds[item] > 0, pair[1:2], pair[0:1])
-        gridded[item] = grid_tile(tiles[item], all_taps[item, 0], all_taps[item, 1].astype(F32), weight)
+    for group in range(0, ROWS, 8):
+        pairs = [got_kept[names[item]].astype(F32) for item in range(group, group + 8)]
+        picked = [jnp.where(seconds[group + item] > 0, pairs[item][1:2], pairs[item][0:1]) for item in range(8)]
+        for item in range(8):
+            tile_weight[group + item] = picked[item]
+
+    def grid_step(group, carry):
+        for place in range(16):
+            item = group * 16 + place
+            gridded[item] = grid_tile(
+                tiles[item], all_taps[item, 0], all_taps[item, 1].astype(F32), tile_weight[item]
+            )
+        return carry
+
+    lax.fori_loop(0, 2, grid_step, 0)
     for pair in range(4):
         gather_pair(pair, gridded, table, twiddle, middle)
     emit_back = emit_fields(fields)
@@ -489,6 +501,7 @@
             pltpu.VMEM((2, 64, EXTENT), F32),
             pltpu.VMEM((PLANES, 2, 64, 256), BF16),
             pltpu.VMEM((ROWS, 2, TILE, V), BF16),
+            pltpu.VMEM((ROWS, 1, V), F32),
             pltpu.VMEM((16, 2, 64, 128), F32),
             pltpu.SMEM((ROWS,), jnp.int32),
             pltpu.SMEM((ROWS,), jnp.int32),

time: 60.4 us -> 56.1 us (0.929)
  Pallas kernels: 57.8 us -> 53.4 us
    pallas_call x1, Pallas kernels: 57.8 us -> 53.4 us  [local(): pl.pallas_call(whole_kernel, out_shape=jax.ShapeDtypeStruct((PLANES, 2, 6...]
where the time goes in v3:
time: 56.1 us; the launch traced here: 55.9 us
  Pallas kernels  53.4 us (95%)
  other arithmetic  1.78 us (3%)
  between operations  0.66 us (1%)
    pallas_call x1, Pallas kernels, local(): pl.pallas_call(whole_kernel, out_shape=jax.ShapeDtypeStruct((PLANES, 2, 6...  53.4 us
    reduce_sum x1, other arithmetic, local(): return jnp.sum(others.astype(F32), axis=0)  1.78 us

profile of v3, /device:TPU:1, one launch (start us, length us, event | category | flops | bytes accessed | tf_op | source)
XLA Modules:
  0.0 55.9 jit_solution(6812531528892146752)
XLA Ops:
  0.7 53.4 %whole.1 = bf16[8,2,64,256]{3,2,1,0:T(8,128)(2,1)} custom-call(f32[1]{0:T(128)S(6)} %copy.9.w_ref, s32[1024]{0:T(1024)} %bitcast.1, s32[1,64]{1,0:T(1,128)} %counts.1, f32[2,64,2048]{2,1,0:T(8,128)} %image_in.1, s32[1,2,64,256]{3,2,1,0:T(8,128)} %positions_in.1, f32[1,64,256]{2,1,0:T(8,128)} %weights_in.1, bf16[512,512]{1,0:T(8,128)(2,1)} %constant.6.clone.table_in, ...), custom_call_target="tpu_custom_call" | custom-call | tf_op jit(solution)/shard_map/whole/pallas_call | solution.py:478
  54.1 1.8 %convert_reduce_fusion = f32[2,64,256]{2,1,0:T(8,128)} fusion(bf16[8,2,64,256]{3,2,1,0:T(8,128)(2,1)} %whole.1), kind=kLoop, calls=%fused_computation | loop fusion | flops 491520 | bytes 655360 | tf_op jit(solution)/shard_map/reduce_sum | solution.py:530

commit v4 on v3

--- a/solution.py
+++ b/solution.py
@@ -252,14 +252,16 @@
 
 def whole_kernel(
     w_ref,
-    owner,
-    counts,
+    owner_in,
+    counts_in,
     image_in,
     positions_in,
     weights_in,
     table_in,
     twiddle_in,
     others,
+    owner,
+    counts,
     image,
     positions,
     weights,
@@ -303,6 +305,8 @@
         pltpu.make_async_copy(source, target, local_sem.at[index])
         for index, (source, target) in enumerate(
             (
+                (owner_in, owner),
+                (counts_in, counts),
                 (image_in, image),
                 (twiddle_in, twiddle),
                 (positions_in, positions),
@@ -334,7 +338,7 @@
         return carry
 
     lax.fori_loop(0, 4, prepare, 0)
-    for copy in loads[0:4]:
+    for copy in loads[0:6]:
         copy.wait()
     place_of = lax.broadcasted_iota(jnp.int32, (1, V), 1)
     for peer in range(ROWS):
@@ -351,10 +355,10 @@
         return carry
 
     lax.fori_loop(0, 4, first_spread, 0)
-    loads[4].wait()
-    turn_blocks(stacked, table, blocks)
     pl.semaphore_wait(barrier, ROWS + PLANES - 2)
     send_all("row", ROWS, me, lambda peer: packed.at[peer], got_packed.at[me], vis_send.at[0], vis_recv.at[0])
+    loads[6].wait()
+    turn_blocks(stacked, table, blocks)
 
     def send_chunk(chunk, carry):
         rows = chunk_rows(chunk)
@@ -478,9 +482,11 @@
     others = pl.pallas_call(
         whole_kernel,
         out_shape=jax.ShapeDtypeStruct((PLANES, 2, 64, 256), BF16),
-        in_specs=[smem] * 3 + [anywhere] * 5,
+        in_specs=[smem] + [pl.BlockSpec(memory_space=pltpu.HBM)] * 7,
         out_specs=anywhere,
         scratch_shapes=[
+            pltpu.SMEM((ROWS * ROWS,), jnp.int32),
+            pltpu.SMEM((1, 64), jnp.int32),
             pltpu.VMEM((2, 64, EXTENT), F32),
             pltpu.VMEM((1, 2, 64, V), jnp.int32),
             pltpu.VMEM((1, 64, V), F32),
@@ -505,7 +511,7 @@
             pltpu.VMEM((16, 2, 64, 128), F32),
             pltpu.SMEM((ROWS,), jnp.int32),
             pltpu.SMEM((ROWS,), jnp.int32),
-            dma((5,)),
+            dma((7,)),
             dma((2,)),
             dma((2,)),
             dma((4,)),
@@ -515,17 +521,22 @@
             dma,
             dma,
         ],
-        compiler_params=pltpu.CompilerParams(collective_id=0, has_side_effects=True),
+        compiler_params=pltpu.CompilerParams(collective_id=0, has_side_effects=True, vmem_limit_bytes=24 * 1024 * 1024),
         name="whole",
     )(
         w_planes,
-        owner.reshape(-1),
-        counts,
-        image,
-        positions,
-        weights,
-        jnp.asarray(table),
-        jnp.asarray(twiddle),
+        *[
+            pltpu.with_memory_space_constraint(value, pltpu.HBM)
+            for value in (
+                owner.reshape(-1),
+                counts,
+                image,
+                positions,
+                weights,
+                jnp.asarray(table),
+                jnp.asarray(twiddle),
+            )
+        ],
     )
     return jnp.sum(others.astype(F32), axis=0)
 

time: 56.1 us -> 54 us (0.963)
  other arithmetic: 1.78 us -> 0.73 us
  Pallas kernels: 53.4 us -> 52.5 us
    reduce_sum x1, other arithmetic: 1.78 us -> 0.73 us  [local(): return jnp.sum(others.astype(F32), axis=0)]
    pallas_call x1, Pallas kernels: 53.4 us -> 52.5 us  [local(): pl.pallas_call(whole_kernel, out_shape=jax.ShapeDtypeStruct((PLANES, 2, 6...]
where the time goes in v4:
time: 54 us; the launch traced here: 53.9 us
  Pallas kernels  52.5 us (97%)
  other arithmetic  0.73 us (1%)
  between operations  0.66 us (1%)
    pallas_call x1, Pallas kernels, local(): pl.pallas_call(whole_kernel, out_shape=jax.ShapeDtypeStruct((PLANES, 2, 6...  52.5 us

profile of v4, /device:TPU:1, one launch (start us, length us, event | category | flops | bytes accessed | tf_op | source)
XLA Modules:
  0.0 53.9 jit_solution(6479428726980835388)
XLA Ops:
  0.7 52.5 %whole.1 = bf16[8,2,64,256]{3,2,1,0:T(8,128)(2,1)S(1)} custom-call(f32[1]{0:T(128)S(6)} %copy.9.w_ref, s32[1024]{0:T(1024)} %bitcast.1, s32[1,64]{1,0:T(1,128)} %counts_in.1, f32[2,64,2048]{2,1,0:T(8,128)} %image_in.1, s32[1,2,64,256]{3,2,1,0:T(8,128)} %positions_in.1, f32[1,64,256]{2,1,0:T(8,128)} %weights_in.1, bf16[512,512]{1,0:T(8,128)(2,1)} %constant.6.clone.table_in, ...), custom_call_target="tpu_custom_call" | custom-call | tf_op jit(solution)/shard_map/whole/pallas_call | solution.py:482
  53.1 0.7 %convert_reduce_fusion = f32[2,64,256]{2,1,0:T(8,128)} fusion(bf16[8,2,64,256]{3,2,1,0:T(8,128)(2,1)S(1)} %whole.1), kind=kLoop, calls=%fused_computation | loop fusion | flops 491520 | bytes 655360 | tf_op jit(solution)/shard_map/reduce_sum | solution.py:541

commit v5 on v4

--- a/solution.py
+++ b/solution.py
@@ -248,6 +248,20 @@
         return carry
 
     lax.fori_loop(1, size, step, 0)
+
+
+def send_planes(plane, terms, others, rows, send, recv):
+    chip, core = plane // 2, lax.rem(plane, 2)
+    for ahead, other in ((2, 0), (2, 1), (1, 0), (3, 0), (1, 1), (3, 1), (0, 1)):
+        peer = lax.rem(chip + ahead, 4) * 2 + lax.rem(core + other, 2)
+        pltpu.make_async_remote_copy(
+            terms.at[peer, :, rows],
+            others.at[plane, :, rows],
+            send,
+            recv,
+            device_id={"plane": peer},
+            device_id_type=MESH,
+        ).start()
 
 
 def whole_kernel(
@@ -426,20 +440,38 @@
         last_block(block, middle, emit_back)
     shuffle_fields(fields, back)
 
-    def back_chunk(chunk, carry):
-        send_all(
-            "row",
-            ROWS,
-            me,
-            lambda peer: back.at[chunk, peer],
+    def back_send_one(peer, chunk):
+        pltpu.make_async_remote_copy(
+            back.at[chunk, peer],
             got_back.at[chunk, me],
             back_send.at[chunk],
             back_recv.at[chunk],
-        )
+            device_id={"row": peer},
+            device_id_type=MESH,
+        ).start()
+
+    for first, second, middle_z, late in ((((0, 1), (0,), (0,), ()), ((2, 3), (1, 2), (1,), (0,)), ((), (3,), (2,), (1,)), ((), (), (3,), (2, 3)))):
+
+        def back_step(offset, carry, first=first, second=second, middle_z=middle_z, late=late):
+            peer = lax.rem(me + offset, ROWS)
+            for chunks, chosen in (
+                (first, peer < 4),
+                (second, (peer >= 4) & (peer < 8)),
+                (middle_z, (peer >= 8) & (peer < 16)),
+                (late, peer >= 16),
+            ):
+                if chunks:
+
+                    @pl.when(chosen)
+                    def _(chunks=chunks):
+                        for chunk in chunks:
+                            back_send_one(peer, chunk)
+
+            return carry
+
+        lax.fori_loop(1, ROWS, back_step, 0)
+    for chunk in range(4):
         got_back[chunk, me] = back[chunk, me]
-        return carry
-
-    lax.fori_loop(0, 4, back_chunk, 0)
 
     def emit(block, rows, half, re, im):
         for a in range(8):
@@ -454,9 +486,7 @@
         gather_chunk(chunk, got_back, table, twiddle, middle)
         last_block(chunk, middle, emit)
         rows = chunk_rows(chunk)
-        send_all(
-            "plane", PLANES, plane, lambda peer: terms.at[peer, :, rows], others.at[plane, :, rows], term_send, term_recv
-        )
+        send_planes(plane, terms, others, rows, term_send, term_recv)
         return carry
 
     lax.fori_loop(0, 4, term_chunk, 0)

time: 54 us -> 51.5 us (0.954)
  the two profiles are of different devices: /device:TPU:1 before, /device:TPU:65 now
where the time goes in v5:
time: 51.5 us; the launch traced here: 51.4 us
  Pallas kernels  50 us (97%)
  other arithmetic  0.73 us (1%)
  between operations  0.66 us (1%)
    pallas_call x1, Pallas kernels, local(): pl.pallas_call(whole_kernel, out_shape=jax.ShapeDtypeStruct((PLANES, 2, 6...  50 us

profile of v5, /device:TPU:65, one launch (start us, length us, event | category | flops | bytes accessed | tf_op | source)
XLA Modules:
  0.0 51.4 jit_solution(3574824320915572723)
XLA Ops:
  0.7 50.0 %whole.1 = bf16[8,2,64,256]{3,2,1,0:T(8,128)(2,1)S(1)} custom-call(f32[1]{0:T(128)S(6)} %copy.9.w_ref, s32[1024]{0:T(1024)} %bitcast.1, s32[1,64]{1,0:T(1,128)} %counts_in.1, f32[2,64,2048]{2,1,0:T(8,128)} %image_in.1, s32[1,2,64,256]{3,2,1,0:T(8,128)} %positions_in.1, f32[1,64,256]{2,1,0:T(8,128)} %weights_in.1, bf16[512,512]{1,0:T(8,128)(2,1)} %constant.6.clone.table_in, ...), custom_call_target="tpu_custom_call" | custom-call | tf_op jit(solution)/shard_map/whole/pallas_call | solution.py:512
  50.7 0.7 %convert_reduce_fusion = f32[2,64,256]{2,1,0:T(8,128)} fusion(bf16[8,2,64,256]{3,2,1,0:T(8,128)(2,1)S(1)} %whole.1), kind=kLoop, calls=%fused_computation | loop fusion | flops 491520 | bytes 655360 | tf_op jit(solution)/shard_map/reduce_sum | solution.py:571

commit v6 on v5

--- a/solution.py
+++ b/solution.py
@@ -241,13 +241,14 @@
 
 
 def greet(axis, size, me, barrier):
-    def step(offset, carry):
+    def step(index, carry):
+        ahead = size // 2 + jnp.where(lax.rem(index, 2) == 1, -((index + 1) // 2), index // 2)
         pl.semaphore_signal(
-            barrier, inc=1, device_id={axis: lax.rem(me + offset, size)}, device_id_type=MESH
+            barrier, inc=1, device_id={axis: lax.rem(me + ahead, size)}, device_id_type=MESH
         )
         return carry
 
-    lax.fori_loop(1, size, step, 0)
+    lax.fori_loop(0, size - 1, step, 0)
 
 
 def send_planes(plane, terms, others, rows, send, recv):
@@ -450,7 +451,7 @@
             device_id_type=MESH,
         ).start()
 
-    for first, second, middle_z, late in ((((0, 1), (0,), (0,), ()), ((2, 3), (1, 2), (1,), (0,)), ((), (3,), (2,), (1,)), ((), (), (3,), (2, 3)))):
+    for first, second, middle_z, late in ((((0, 1), (0,), (0,), ()), ((2, 3), (1, 2), (1,), (0,)), ((), (3,), (2, 3), (1, 2)), ((), (), (), (3,)))):
 
         def back_step(offset, carry, first=first, second=second, middle_z=middle_z, late=late):
             peer = lax.rem(me + offset, ROWS)

time: 51.5 us -> 51.2 us (level)
  no operation moved by 1% of the time
where the time goes in v6:
time: 51.2 us; the launch traced here: 51.1 us
  Pallas kernels  49.7 us (97%)
  other arithmetic  0.73 us (1%)
  between operations  0.66 us (1%)
    pallas_call x1, Pallas kernels, local(): pl.pallas_call(whole_kernel, out_shape=jax.ShapeDtypeStruct((PLANES, 2, 6...  49.7 us

profile of v6, /device:TPU:65, one launch (start us, length us, event | category | flops | bytes accessed | tf_op | source)
XLA Modules:
  0.0 51.1 jit_solution(8704363621246793923)
XLA Ops:
  0.7 49.7 %whole.1 = bf16[8,2,64,256]{3,2,1,0:T(8,128)(2,1)S(1)} custom-call(f32[1]{0:T(128)S(6)} %copy.9.w_ref, s32[1024]{0:T(1024)} %bitcast.1, s32[1,64]{1,0:T(1,128)} %counts_in.1, f32[2,64,2048]{2,1,0:T(8,128)} %image_in.1, s32[1,2,64,256]{3,2,1,0:T(8,128)} %positions_in.1, f32[1,64,256]{2,1,0:T(8,128)} %weights_in.1, bf16[512,512]{1,0:T(8,128)(2,1)} %constant.6.clone.table_in, ...), custom_call_target="tpu_custom_call" | custom-call | tf_op jit(solution)/shard_map/whole/pallas_call | solution.py:513
  50.4 0.7 %convert_reduce_fusion = f32[2,64,256]{2,1,0:T(8,128)} fusion(bf16[8,2,64,256]{3,2,1,0:T(8,128)(2,1)S(1)} %whole.1), kind=kLoop, calls=%fused_computation | loop fusion | flops 491520 | bytes 655360 | tf_op jit(solution)/shard_map/reduce_sum | solution.py:572

commit v7 on v6

--- a/solution.py
+++ b/solution.py
@@ -181,8 +181,8 @@
 def emit_fields(fields):
     def emit(block, rows, half, re, im):
         for a in range(8):
-            fields[2 * a + half, 0, rows, :] = re[a]
-            fields[2 * a + half, 1, rows, :] = im[a]
+            fields[2 * a + half, 0, rows, :] = re[a].astype(BF16)
+            fields[2 * a + half, 1, rows, :] = im[a].astype(BF16)
 
     return emit
 
@@ -199,7 +199,7 @@
                     parts[index] = jnp.where(low, first, pltpu.roll(second, shift, 1))
                     parts[index + bit] = jnp.where(low, pltpu.roll(first, 128 - shift, 1), second)
         for index in range(8):
-            back[index % 4, 2 * column + index // 4] = parts[index].astype(BF16)
+            back[index % 4, 2 * column + index // 4] = parts[index]
 
 
 def taps_of(position, places):
@@ -539,7 +539,7 @@
             pltpu.VMEM((PLANES, 2, 64, 256), BF16),
             pltpu.VMEM((ROWS, 2, TILE, V), BF16),
             pltpu.VMEM((ROWS, 1, V), F32),
-            pltpu.VMEM((16, 2, 64, 128), F32),
+            pltpu.VMEM((16, 2, 64, 128), BF16),
             pltpu.SMEM((ROWS,), jnp.int32),
             pltpu.SMEM((ROWS,), jnp.int32),
             dma((7,)),

time: 51.2 us -> 51.3 us (level)
  no operation moved by 1% of the time
where the time goes in v7:
time: 51.3 us; the launch traced here: 51.2 us
  Pallas kernels  49.8 us (97%)
  other arithmetic  0.73 us (1%)
  between operations  0.66 us (1%)
    pallas_call x1, Pallas kernels, local(): pl.pallas_call(whole_kernel, out_shape=jax.ShapeDtypeStruct((PLANES, 2, 6...  49.8 us

profile of v7, /device:TPU:65, one launch (start us, length us, event | category | flops | bytes accessed | tf_op | source)
XLA Modules:
  0.0 51.2 jit_solution(10334179760938269441)
XLA Ops:
  0.7 49.8 %whole.1 = bf16[8,2,64,256]{3,2,1,0:T(8,128)(2,1)S(1)} custom-call(f32[1]{0:T(128)S(6)} %copy.9.w_ref, s32[1024]{0:T(1024)} %bitcast.1, s32[1,64]{1,0:T(1,128)} %counts_in.1, f32[2,64,2048]{2,1,0:T(8,128)} %image_in.1, s32[1,2,64,256]{3,2,1,0:T(8,128)} %positions_in.1, f32[1,64,256]{2,1,0:T(8,128)} %weights_in.1, bf16[512,512]{1,0:T(8,128)(2,1)} %constant.6.clone.table_in, ...), custom_call_target="tpu_custom_call" | custom-call | tf_op jit(solution)/shard_map/whole/pallas_call | solution.py:513
  50.4 0.7 %convert_reduce_fusion = f32[2,64,256]{2,1,0:T(8,128)} fusion(bf16[8,2,64,256]{3,2,1,0:T(8,128)(2,1)S(1)} %whole.1), kind=kLoop, calls=%fused_computation | loop fusion | flops 491520 | bytes 655360 | tf_op jit(solution)/shard_map/reduce_sum | solution.py:572
